TPU v7x, 32 devices: a whole 2x2x4 slice. The times are simulated.
32 devices in a mesh: sec: 4 (over x, core), lat: 2 (over y), col: 4 (over z).
Axes of the slice: x: 2, y: 2, z: 4, core: 2. Of those that a mesh axis runs over, the one named last changes fastest.
Arguments:
- state: float32 [1, 4, 28, 192, 384], P(None, 'sec', None, 'lat', 'col'), may hold values from -6 to 6
- forcing: float32 [1, 4, 28, 192, 384], P(None, 'sec', None, 'lat', 'col'), may hold values from -4 to 4
- crm_moisture: bfloat16 [1, 32, 28, 8, 4, 2304], P(None, None, None, ('sec', 'lat'), 'col'), may hold values from -6 to 6
- cloud_order: int32 [4, 2, 9216], P('col', 'lat'), may hold values from 0 to 9215, each once within a row
- wave_table: int32 [128], replicated, may hold values from 0 to 127, each once
Outputs:
- state_out: float32 [1, 4, 28, 192, 384], P(None, 'sec', None, 'lat', 'col')
- spectral: float32 [4, 1, 28, 128, 2, 128], P('sec', None, 'col', 'lat')
Inputs may be any that keep to these rules, and one draw needn't show every extreme that they name: `cloud_order`: every row lists each of the 9216 columns of a band block once. `wave_table`: each wavenumber stands in exactly one slot.
All inputs are finite; a program needn't handle non-finite values.
Results may differ from a plain program's by a relative error of at most 0.0003.
Values sent between devices are 32-bit elements; how exact they have to be, the bound alone decides.
A program may use at most 128 MiB of HBM per device.

v0:
```python
import math
import jax
import jax.numpy as jnp
from jax import lax
from jax.sharding import PartitionSpec as P

NLON = 384
NLAT = 192
MMAX = 128
NSUB = 4
COURANT_SCALE = 0.4
CONDENSE = 0.5


def transport(values, courant, mixing):
    forward = jnp.roll(values, -1, axis=0)
    behind = jnp.roll(values, 1, axis=0)
    return -0.5 * courant * (forward - behind) + mixing * (forward - 2.0 * values + behind)


def cloud_model(vertical_state_stack, forcing, vapour_mass_fraction):
    wind_u = vertical_state_stack[0]
    wind_v = vertical_state_stack[1]
    atmospheric_warmth = vertical_state_stack[2]
    humidity = vertical_state_stack[3]
    courant = COURANT_SCALE * jnp.tanh(wind_u)
    mixing = 0.2 + 0.5 * jnp.abs(courant)
    convective_warming_rate = jnp.broadcast_to(atmospheric_warmth, vapour_mass_fraction.shape)
    crm_water = humidity + vapour_mass_fraction
    start_water = crm_water
    ground_precipitation = jnp.zeros_like(atmospheric_warmth)
    for substep in range(NSUB):
        heat_move = transport(convective_warming_rate, courant, mixing)
        water_move = transport(crm_water, courant, mixing)
        condensed = CONDENSE * jnp.maximum(crm_water - convective_warming_rate, 0.0)
        convective_warming_rate = (
            convective_warming_rate + heat_move + condensed + forcing[2] / NSUB
        )
        crm_water = crm_water + water_move - condensed + forcing[3] / NSUB
        ground_precipitation = ground_precipitation + jnp.mean(condensed, axis=0)
    ground_precipitation = ground_precipitation / NSUB
    zonal_velocity_rate = -ground_precipitation * wind_u + forcing[0]
    meridional_velocity_rate = -ground_precipitation * wind_v + forcing[1]
    warming_rate_change = jnp.mean(convective_warming_rate, axis=0) - atmospheric_warmth
    vapour_rate_change = jnp.mean(crm_water - start_water, axis=0)
    return jnp.stack(
        (zonal_velocity_rate, meridional_velocity_rate, warming_rate_change, vapour_rate_change)
    )


def trig_table(longitudes, wave_numbers):
    phase = (longitudes[:, None] * wave_numbers[None, :] % NLON).astype(jnp.float32) * (
        2.0 * math.pi / NLON
    )
    return jnp.stack((jnp.cos(phase), jnp.sin(phase)), axis=1) / math.sqrt(NLON)


def legendre_table(orders):
    colatitude = (jnp.arange(NLAT, dtype=jnp.int32).astype(jnp.float32) + 0.5) * (math.pi / NLAT)
    cosine = jnp.cos(colatitude)[None, :]
    sine_lat = jnp.sin(colatitude)
    order_col = orders.astype(jnp.float32)[:, None]
    log_diag = 0.5 * (
        lax.lgamma(order_col + 1.5) - lax.lgamma(jnp.float32(1.5)) - lax.lgamma(order_col + 1.0)
    )
    log_diag = log_diag + order_col * jnp.log(sine_lat)[None, :] - 0.5 * math.log(2.0)
    diagonal = jnp.exp(log_diag)
    empty = jnp.zeros_like(diagonal)

    def march_forward(carried, degree):
        previous, current = carried
        deg_float = degree.astype(jnp.float32)
        active = deg_float > order_col
        numerator = jnp.where(active, 4.0 * deg_float * deg_float - 1.0, 1.0)
        bottom = jnp.where(active, deg_float * deg_float - order_col * order_col, 1.0)
        lower_deg = deg_float - 1.0
        retreat = jnp.sqrt(
            jnp.maximum(lower_deg * lower_deg - order_col * order_col, 0.0)
            / (4.0 * lower_deg * lower_deg - 1.0)
        )
        grown = jnp.sqrt(numerator / bottom) * (cosine * current - retreat * previous)
        fresh_row = jnp.where(active, grown, jnp.where(deg_float == order_col, diagonal, 0.0))
        return ((current, fresh_row), fresh_row)

    _, legendre_rows = lax.scan(
        march_forward, (empty, empty), jnp.arange(MMAX, dtype=jnp.int32), unroll=8
    )
    weights = sine_lat / math.sqrt(NLAT)
    return legendre_rows * weights[None, None, :]


def shards(state, forcing, crm_moisture, cloud_order, wave_table):
    members, _, levels, band_rows, lon_block = state.shape
    sections = lax.axis_size("sec")
    lat_bands = lax.axis_size("lat")
    block_cols = band_rows * lon_block
    targets = sections * lat_bands
    per_target = block_cols // targets
    run_cols = lat_bands * per_target
    slot_list = cloud_order[0, 0]
    flat_state = state[:, 0].reshape(members, levels, block_cols)
    flat_force = forcing[:, 0].reshape(members, levels, block_cols)
    stacked = jnp.stack((flat_state, flat_force))
    use_matrix = block_cols <= 2048
    if use_matrix:
        column_ids = jnp.arange(block_cols, dtype=jnp.int32)
        selector = (slot_list[:, None] == column_ids[None, :]).astype(jnp.float32)
        selector = selector.reshape(targets, per_target, block_cols)
        by_target = jnp.einsum(
            "xelc,tpc->txelp", stacked, selector, precision=lax.Precision.HIGHEST
        )
    else:
        slot_table = slot_list.reshape(targets, per_target)
        by_target = jnp.take(stacked, slot_table, axis=3).transpose(3, 0, 1, 2, 4)
    send_width = 2 * members * levels * per_target
    outgoing = by_target.reshape(targets, 1, send_width)
    arrived = lax.all_to_all(outgoing, ("sec", "lat"), split_axis=0, concat_axis=1, tiled=True)
    arrived = arrived.reshape(sections, lat_bands, 2, members, levels, per_target)
    arrived = arrived.transpose(2, 3, 0, 4, 1, 5).reshape(2, members, sections, levels, run_cols)
    vapour_mass_fraction = crm_moisture[:, :, :, 0, 0, :].astype(jnp.float32)
    tendency = jax.vmap(cloud_model)(arrived[0], arrived[1], vapour_mass_fraction)
    back_width = members * levels * per_target
    parted = tendency.reshape(members, sections, levels, lat_bands, per_target).transpose(
        1, 3, 0, 2, 4
    )
    homeward = parted.reshape(targets, 1, back_width)
    returned = lax.all_to_all(homeward, ("sec", "lat"), split_axis=0, concat_axis=1, tiled=True)
    returned = returned.reshape(targets, members, levels, per_target)
    if use_matrix:
        column_tend = jnp.einsum(
            "telp,tpc->elc", returned, selector, precision=lax.Precision.HIGHEST
        )
    else:
        in_slot_order = returned.transpose(1, 2, 0, 3).reshape(members, levels, block_cols)
        inverse = (
            jnp.zeros((block_cols,), jnp.int32)
            .at[slot_list]
            .set(jnp.arange(block_cols, dtype=jnp.int32))
        )
        column_tend = jnp.take(in_slot_order, inverse, axis=2)
    new_state = state + column_tend.reshape(members, 1, levels, band_rows, lon_block)
    fields_now = new_state[:, 0]
    regrouped = lax.all_to_all(fields_now, "col", split_axis=1, concat_axis=3, tiled=True)
    trig_rows = trig_table(jnp.arange(NLON, dtype=jnp.int32), wave_table)
    spectra = jnp.einsum("elay,ycs->leacs", regrouped, trig_rows, precision=lax.Precision.HIGHEST)
    owner_count = MMAX // lat_bands
    owned_waves = lax.dynamic_slice_in_dim(
        wave_table, lax.axis_index("lat") * owner_count, owner_count
    )
    weighted = legendre_table(owned_waves)
    coeffs = jnp.einsum(
        "leacs,nsa->lescn",
        lax.all_to_all(spectra, "lat", split_axis=4, concat_axis=2, tiled=True),
        weighted,
        precision=lax.Precision.HIGHEST,
    )
    return (new_state, coeffs.transpose(1, 0, 2, 3, 4)[None])


def solution(mesh):
    placed = (
        P(None, "sec", None, "lat", "col"),
        P(None, "sec", None, "lat", "col"),
        P(None, None, None, ("sec", "lat"), "col", None),
        P("col", "lat", None),
        P(),
    )
    return jax.shard_map(
        shards,
        mesh=mesh,
        in_specs=placed,
        out_specs=(P(None, "sec", None, "lat", "col"), P("sec", None, "col", "lat", None, None)),
        check_vma=False,
    )
```

profile of v0, /device:TPU:0, one launch (start us, length us, event | category | flops | bytes accessed | tf_op | source)
XLA Modules:
  0.0 617.8 jit_solution(15308398719967561475)
XLA Ops:
  0.6 4.0 copy.116
  4.6 4.0 copy.117
  8.7 13.0 %maximum_bitcast_fusion = f32[2,28,9216]{1,0,2:T(2,128)} fusion(f32[1,1,28,9216]{2,0,3,1:T(1,128)} %bitcast.285, f32[1,1,28,9216]{2,0,3,1:T(1,128)} %bitcast.284), kind=kLoop, calls=%fused_computation.84 | loop fusion | flops 516096 | bytes 4128768 | tf_op jit(solution)/shard_map/stack | solution.py:103
  21.7 66.6 %gather_fusion = f32[9216,2,28]{2,1,0:T(2,128)} fusion(f32[2,28,9216]{1,0,2:T(2,128)} %maximum_bitcast_fusion, s32[9216]{0:T(1024)S(1)} %broadcast_clamp_fusion), kind=kCustom, calls=%fused_computation | custom fusion | bytes 4165632 | tf_op jit(solution)/shard_map/jit(_take)/gather | solution.py:114
  88.3 8.0 %copy.118 = f32[8,1152,2,28]{1,0,2,3:T(8,128)S(1)} copy(f32[8,1152,2,28]{3,2,1,0:T(2,128)} %bitcast.286) | data formatting | bytes 4128768 | tf_op jit(solution)/shard_map/jit(_take)/gather | solution.py:114
  97.9 2.1 copy.96
  100.1 30.3 %all_to_all.48 = f32[8,1,64512]{2,1,0:T(1,128)S(1)} all-to-all(f32[8,1,64512]{2,1,0:T(1,128)S(1)} %copy.96), channel_id=1, replica_groups=mesh['sec'=4,'lat'=2,'col'=4] {'sec','lat'}, dimensions={0} | all-to-all | bytes 4128768 | tf_op jit(solution)/shard_map/all_to_all | solution.py:117
  130.4 6.9 %reduce.8 = f32[8,64512]{1,0:T(8,128)} reduce(f32[8,1,64512]{2,1,0:T(1,128)S(1)} %all_to_all.48, f32[]{:T(128)} %constant.239), dimensions={1}, to_apply=%all_to_all.16.reduce_sub_computation | reduce | bytes 4128772 | tf_op jit(solution)/shard_map/all_to_all | solution.py:117
  137.3 2.0 reshape.4359
  140.3 1.0 squeeze.69
  141.3 1.8 broadcast_multiply_fusion.3
  143.9 1.8 copy.98
  145.7 2.2 squeeze.70
  147.9 0.9 slice_multiply_fusion.1
  148.9 1.8 copy_bitcast_fusion.3
  151.4 8.7 %fusion.44 = (f32[1,32,28,2304]{3,1,2,0:T(8,128)}, f32[1,32,28,2304]{3,1,2,0:T(8,128)S(1)}) fusion(f32[1,1,28,2304]{3,1,2,0:T(1,128)S(1)} %get-tuple-element.412, f32[1,31,28,2304]{3,1,2,0:T(8,128)S(1)} %slice.206, bf16[1,32,28,1,1,2304]{5,1,4,3,2,0:T(8,128)(2,1)S(1)} %copy-done.2, f32[28,2304]{1,0:T(8,128)S(1)} %get-tuple-element.418, ...), kind=kLoop, calls=%fused_computation.94 | loop fusion | flops 33030144 | bytes 30449664 | tf_op jit(solution)/shard_map/vmap()/add | solution.py:37
  160.0 6.5 %fusion.107 = (f32[1,31,28,2304]{3,1,2,0:T(8,128)}, f32[1,31,28,2304]{3,1,2,0:T(8,128)}) fusion(f32[1,32,28,2304]{3,1,2,0:T(8,128)S(1)} %get-tuple-element.407), kind=kLoop, calls=%fused_computation.237 | loop fusion | bytes 31997952 | tf_op jit(solution)/shard_map/vmap(jit(_roll_static))/slice | solution.py:16
  166.9 15.7 %fusion.51 = (f32[28,2304]{1,0:T(8,128)}, f32[28,2304]{1,0:T(8,128)}, f32[1,32,28,2304]{3,1,2,0:T(8,128)S(1)}) fusion(f32[28,2304]{1,0:T(8,128)S(1)} %get-tuple-element.418, bf16[1,32,28,1,1,2304]{5,1,4,3,2,0:T(8,128)(2,1)S(1)} %copy-done.2, f32[28,2304]{1,0:T(8,128)S(1)} %get-tuple-element.423, f32[28,2304]{1,0:T(8,128)S(1)} %copy-done.8, ...), kind=kLoop, calls=%fused_computation.125 | loop fusion | flops 67995648 | bytes 39481344 | tf_op jit(solution)/shard_map/vmap()/reduce_sum | solution.py:40
  182.5 8.4 %fusion.105 = (f32[1,31,28,2304]{3,1,2,0:T(8,128)}, f32[1,31,28,2304]{3,1,2,0:T(8,128)}) fusion(f32[1,32,28,2304]{3,1,2,0:T(8,128)S(1)} %get-tuple-element.336), kind=kLoop, calls=%fused_computation.235 | loop fusion | bytes 31997952 | tf_op jit(solution)/shard_map/vmap(jit(_roll_static))/slice | solution.py:16
  190.9 2.2 copy-done
  193.2 1.2 fusion.106
  194.3 6.4 %fusion.103 = (f32[1,31,28,2304]{3,1,2,0:T(8,128)}, f32[1,31,28,2304]{3,1,2,0:T(8,128)}) fusion(f32[1,32,28,2304]{3,1,2,0:T(8,128)S(1)} %bitcast.282), kind=kLoop, calls=%fused_computation.233 | loop fusion | bytes 31997952 | tf_op jit(solution)/shard_map/vmap(jit(_roll_static))/slice | solution.py:16
  200.7 1.2 fusion.104
  201.9 31.2 %fusion.52 = (f32[28,2304]{1,0:T(8,128)}, f32[1,32,28,2304]{3,1,2,0:T(8,128)}, f32[1,32,28,2304]{3,1,2,0:T(8,128)}) fusion(f32[28,2304]{1,0:T(8,128)S(1)} %get-tuple-element.419, f32[1,32,28,2304]{3,1,2,0:T(8,128)} %copy-done, f32[28,2304]{1,0:T(8,128)S(1)} %get-tuple-element.418, bf16[1,32,28,1,1,2304]{5,1,4,3,2,0:T(8,128)(2,1)S(1)} %copy-done.2, ...), kind=kLoop, calls=%fused_computation.126 | loop fusion | flops 96961536 | bytes 72253440 | tf_op jit(solution)/shard_map/vmap()/reduce_sum | solution.py:40
  233.0 12.5 %fusion.97 = (f32[1,31,28,2304]{3,1,2,0:T(8,128)}, f32[1,31,28,2304]{3,1,2,0:T(8,128)}) fusion(f32[1,32,28,2304]{3,1,2,0:T(8,128)} %get-tuple-element.338), kind=kLoop, calls=%fused_computation.227 | loop fusion | bytes 31997952 | tf_op jit(solution)/shard_map/vmap(jit(_roll_static))/slice | solution.py:16
  245.5 3.4 fusion.98
  248.9 6.4 %fusion.101 = (f32[1,31,28,2304]{3,1,2,0:T(8,128)}, f32[1,31,28,2304]{3,1,2,0:T(8,128)}) fusion(f32[1,32,28,2304]{3,1,2,0:T(8,128)S(1)} %bitcast.280), kind=kLoop, calls=%fused_computation.231 | loop fusion | bytes 31997952 | tf_op jit(solution)/shard_map/vmap(jit(_roll_static))/slice | solution.py:16
  255.3 1.1 fusion.102
  256.4 18.1 %subtract_add_fusion = (f32[1,32,28,2304]{3,1,2,0:T(8,128)S(1)}, f32[1,32,28,2304]{3,1,2,0:T(8,128)S(1)}) fusion(f32[1,32,28,2304]{3,1,2,0:T(8,128)} %get-tuple-element.338, f32[1,31,28,2304]{3,1,2,0:T(8,128)} %get-tuple-element.383, f32[1,1,28,2304]{3,1,2,0:T(1,128)} %get-tuple-element.385, f32[1,1,28,2304]{3,1,2,0:T(1,128)} %get-tuple-element.384, ...), kind=kLoop, calls=%fused_computation.114 | loop fusion | flops 55738368 | bytes 67092480 | tf_op jit(solution)/shard_map/vmap()/add | solution.py:39
  274.5 6.4 %fusion.95 = (f32[1,31,28,2304]{3,1,2,0:T(8,128)}, f32[1,31,28,2304]{3,1,2,0:T(8,128)}) fusion(f32[1,32,28,2304]{3,1,2,0:T(8,128)S(1)} %get-tuple-element.376), kind=kLoop, calls=%fused_computation.225 | loop fusion | bytes 31997952 | tf_op jit(solution)/shard_map/vmap(jit(_roll_static))/slice | solution.py:16
  280.9 1.1 fusion.96
  282.0 6.4 %fusion.99 = (f32[1,31,28,2304]{3,1,2,0:T(8,128)}, f32[1,31,28,2304]{3,1,2,0:T(8,128)}) fusion(f32[1,32,28,2304]{3,1,2,0:T(8,128)S(1)} %get-tuple-element.377), kind=kLoop, calls=%fused_computation.229 | loop fusion | bytes 31997952 | tf_op jit(solution)/shard_map/vmap(jit(_roll_static))/slice | solution.py:16
  288.4 1.2 fusion.100
  289.6 20.4 %add_reduce_fusion = (f32[28,2304]{1,0:T(8,128)}, f32[28,2304]{1,0:T(8,128)}, f32[28,2304]{1,0:T(8,128)}) fusion(f32[1,32,28,2304]{3,1,2,0:T(8,128)S(1)} %get-tuple-element.377, f32[1,31,28,2304]{3,1,2,0:T(8,128)} %get-tuple-element.387, f32[1,1,28,2304]{3,1,2,0:T(1,128)} %get-tuple-element.389, f32[1,1,28,2304]{3,1,2,0:T(1,128)} %get-tuple-element.388, ...), kind=kLoop, calls=%fused_computation.111 | loop fusion | flops 67931136 | bytes 55738368 | tf_op jit(solution)/shard_map/vmap()/reduce_sum | solution.py:44
  310.0 1.0 broadcast_multiply_fusion.1
  311.0 1.3 multiply_negate_fusion
  312.3 4.1 fusion.64
  317.3 2.0 reshape.4406
  319.3 3.6 all-to-all-start.1
  322.9 34.2 %scatter_custom_fusion = s32[9216]{0:T(1024)S(1)} fusion(s32[9216]{0:T(1024)S(1)} %bitcast.309, s32[9216]{0:T(1024)S(1)} %iota.45, s32[]{:T(128)} %constant.186.clone.1), kind=kCustom, calls=%fused_computation.179 | custom fusion | bytes 36868 | tf_op jit(solution)/shard_map/scatter | solution.py:138
  357.4 3.4 copy.105
  360.8 33.4 %gather_fusion.1 = f32[9216,28]{1,0:T(8,128)} fusion(f32[28,9216]{0,1:T(8,128)} %bitcast.283, s32[9216]{0:T(1024)S(1)} %fusion.73), kind=kCustom, calls=%fused_computation.1 | custom fusion | bytes 2101248 | tf_op jit(solution)/shard_map/jit(_take)/gather | solution.py:140
  394.2 3.2 copy.106
  397.4 1.3 select_add_fusion
  398.7 5.1 all-to-all-start.2
  405.4 31.7 %all-to-all-done.2 = f32[1,28,96,96]{3,2,0,1:T(8,128)S(1)} async-done(((f32[1,28,96,96]{3,2,0,1:T(8,128)}), f32[1,28,96,96]{3,2,0,1:T(8,128)S(1)}, u32[]{:S(2)}, u32[]{:S(2)}) %all-to-all-start.2) | async-done | bytes 1032224 | tf_op jit(solution)/shard_map/all_to_all | solution.py:143
  437.1 0.9 copy.136
  438.7 1.3 convolution_bitcast_fusion
  440.0 1.4 copy.109
  441.4 3.6 all-to-all-start.3
  444.9 153.6 %while.19 = (s32[]{:T(128)}, f32[64,192]{1,0:T(8,128)S(1)}, f32[64,192]{1,0:T(8,128)S(1)}, f32[16,8,64,192]{3,2,1,0:T(8,128)}, s32[16,8]{0,1:T(8,128)S(1)}, /*in...) while((s32[]{:T(128)}, f32[64,192]{1,0:T(8,128)S(1)}, ...), condition=%wide.region_8.9_spmd.clone.clone, body=%wide.region_7.8_spmd.clone.clone.sunk | while | flops 926866 | bytes 3029748 | solution.py:85
  463.3 0.9 bitcast_dynamic-update-slice_fusion.26
  482.5 0.9 bitcast_dynamic-update-slice_fusion.26
  492.0 0.9 bitcast_dynamic-update-slice_fusion.26
  520.8 0.9 bitcast_dynamic-update-slice_fusion.26
  530.4 0.9 bitcast_dynamic-update-slice_fusion.26
  540.0 0.9 bitcast_dynamic-update-slice_fusion.26
  559.2 0.9 bitcast_dynamic-update-slice_fusion.26
  568.8 0.9 bitcast_dynamic-update-slice_fusion.26
  588.0 0.9 bitcast_dynamic-update-slice_fusion.26
  597.7 0.9 bitcast_dynamic-update-slice_fusion.26
  598.5 8.6 %copy.107 = f32[128,64,192]{0,2,1:T(8,128)} copy(f32[128,64,192]{2,1,0:T(8,128)} %bitcast.288) | data formatting | bytes 12582912 | tf_op jit(solution)/shard_map/reshape | solution.py:85
  608.6 7.7 %fusion.56 = f32[1,1,7,64,2,128]{5,2,4,3,1,0:T(8,128)S(1)} fusion(f32[7,192,2,64]{1,0,2,3:T(8,128)S(1)} %reshape.4408, f32[128,64,192]{0,2,1:T(8,128)} %copy.107, f32[192]{0:T(256)S(1)} %fusion.76), kind=kOutput, calls=%fused_computation.134 | convolution fusion | flops 265814016 | bytes 7439104 | tf_op jit(solution)/shard_map/leacs,nsa->lescn/dot_general | solution.py:151
  616.4 1.0 copy.113
  (331 shorter events, 72.7 us)
Async XLA Ops:
  0.6 8.1 %copy-start.11 = (s32[1,1,9216]{2,1,0:T(1,128)S(1)}, s32[1,1,9216]{2,1,0:T(1,128)}, u32[]{:S(2)}) copy-start(s32[1,1,9216]{2,1,0:T(1,128)} %param.10) | copy-start | bytes 110596
  141.3 2.6 copy-start.5
  143.9 58.0 %copy-start.3 = (f32[28,2304]{1,0:T(8,128)}, f32[28,2304]{1,0:T(8,128)S(1)}, u32[]{:S(2)}) copy-start(f32[28,2304]{1,0:T(8,128)S(1)} %get-tuple-element.423) | copy-start | bytes 774148
  143.9 7.5 %copy-start.8 = (f32[28,2304]{1,0:T(8,128)S(1)}, f32[28,2304]{1,0:T(8,128)}, u32[]{:S(2)}) copy-start(f32[28,2304]{1,0:T(8,128)} %broadcast_multiply_fusion.2) | copy-start | bytes 774148
  147.9 1.0 copy-start.9
  147.9 3.5 copy-start.2
  151.3 15.5 %copy-start.1 = (f32[1,31,28,2304]{3,1,2,0:T(8,128)}, f32[1,31,28,2304]{3,1,2,0:T(8,128)S(1)}, u32[]{:S(2)}) copy-start(f32[1,31,28,2304]{3,1,2,0:T(8,128)S(1)} %slice.206) | copy-start | bytes 23998468
  182.5 10.6 %copy-start = (f32[1,32,28,2304]{3,1,2,0:T(8,128)}, f32[1,32,28,2304]{3,1,2,0:T(8,128)S(1)}, u32[]{:S(2)}) copy-start(f32[1,32,28,2304]{3,1,2,0:T(8,128)S(1)} %get-tuple-element.336) | copy-start | bytes 24772612
  182.5 11.8 %slice-start.2 = ((s8[8257536]{0:T(1024)(128)(4,1)}), s8[4194304]{0:T(1024)(128)(4,1)S(1)}, s32[]{:S(2)}) async-start(s8[8257536]{0:T(1024)(128)(4,1)} %bitcast.281), calls=%async_computation.6 | async-start | bytes 8388608
  182.5 11.8 %slice-start.3 = ((s8[8257536]{0:T(1024)(128)(4,1)}), s8[4063232]{0:T(1024)(128)(4,1)S(1)}, s32[]{:S(2)}) async-start(s8[8257536]{0:T(1024)(128)(4,1)} %bitcast.281), calls=%async_computation.7 | async-start | bytes 8126464
  233.0 15.9 %slice-start = ((s8[8257536]{0:T(1024)(128)(4,1)}), s8[4194304]{0:T(1024)(128)(4,1)S(1)}, s32[]{:S(2)}) async-start(s8[8257536]{0:T(1024)(128)(4,1)} %bitcast.279), calls=%async_computation.4 | async-start | bytes 8388608
  233.0 15.9 %slice-start.1 = ((s8[8257536]{0:T(1024)(128)(4,1)}), s8[4063232]{0:T(1024)(128)(4,1)S(1)}, s32[]{:S(2)}) async-start(s8[8257536]{0:T(1024)(128)(4,1)} %bitcast.279), calls=%async_computation.5 | async-start | bytes 8126464
  282.0 7.6 %copy-start.4 = (f32[28,2304]{1,0:T(8,128)S(1)}, f32[28,2304]{1,0:T(8,128)}, u32[]{:S(2)}) copy-start(f32[28,2304]{1,0:T(8,128)} %copy-done.3) | copy-start | bytes 774148
  289.6 22.7 %copy-start.6 = (f32[1,4,28,2304]{3,1,2,0:T(4,128)S(1)}, f32[1,4,28,2304]{3,1,2,0:T(4,128)}, u32[]{:S(2)}) copy-start(f32[1,4,28,2304]{3,1,2,0:T(4,128)} %copy-done.5) | copy-start | bytes 3096580
  310.0 7.0 %copy-start.10 = (f32[28,2304]{1,0:T(8,128)S(1)}, f32[28,2304]{1,0:T(8,128)}, u32[]{:S(2)}) copy-start(f32[28,2304]{1,0:T(8,128)} %get-tuple-element.275) | copy-start | bytes 774148
  310.0 12.9 %copy-start.12 = (s32[1,1,9216]{2,1,0:T(1,128)S(1)}, s32[1,1,9216]{2,1,0:T(1,128)}, u32[]{:S(2)}) copy-start(s32[1,1,9216]{2,1,0:T(1,128)} %param.10) | copy-start | bytes 110596
  319.3 38.0 %all-to-all-start.1 = ((f32[8,1,32256]{2,1,0:T(1,128)}), f32[8,1,32256]{2,1,0:T(1,128)S(1)}, u32[]{:S(2)}, u32[]{:S(2)}) async-start(f32[8,1,32256]{2,1,0:T(1,128)} %reshape.4406), calls=%async_computation.1 | async-start | bytes 2064384 | tf_op jit(solution)/shard_map/all_to_all | solution.py:127
  360.8 36.6 %copy-start.7 = (f32[1,1,28,96,96]{4,3,2,1,0:T(8,128)S(1)}, f32[1,1,28,96,96]{4,3,2,1,0:T(8,128)}, u32[]{:S(2)}) copy-start(f32[1,1,28,96,96]{4,3,2,1,0:T(8,128)} %param.7) | copy-start | bytes 3096580
  394.2 9.7 %copy-start.13 = (s32[128]{0:T(128)S(1)}, s32[128]{0:T(128)}, u32[]{:S(2)}) copy-start(s32[128]{0:T(128)} %param.11) | copy-start | bytes 1540
  398.7 38.4 %all-to-all-start.2 = ((f32[1,28,96,96]{3,2,0,1:T(8,128)}), f32[1,28,96,96]{3,2,0,1:T(8,128)S(1)}, u32[]{:S(2)}, u32[]{:S(2)}) async-start(f32[1,28,96,96]{3,2,0,1:T(8,128)} %bitcast.25), calls=%async_computation.2 | async-start | bytes 2752512 | tf_op jit(solution)/shard_map/all_to_all | solution.py:143
  441.4 165.8 %all-to-all-start.3 = ((f32[7,1,96,2,128]{2,3,1,0,4:T(2,128)}), f32[7,1,96,2,128]{2,3,1,0,4:T(2,128)S(1)}, u32[]{:S(2)}, u32[]{:S(2)}) async-start(f32[7,1,96,2,128]{2,3,1,0,4:T(2,128)} %copy.109), calls=%async_computation.3 | async-start | bytes 1835008 | tf_op jit(solution)/shard_map/all_to_all | solution.py:153
where the time goes:
time: 625 us; the launch traced here: 618 us
  local copies, waits for them, and re-layouts  276 us (44%)
  other arithmetic  175 us (28%)
  loops' own time  81.3 us (13%)
  waiting for transfers between devices  31.7 us (5%)
  blocking collectives  30.3 us (5%)
  starting transfers between devices  12.2 us (2%)
  matrix products  9.01 us (1%)
    another operation x1, loops' own time, legendre_table(): lax.scan(march_forward, (empty, empty), jnp.arange(MMAX, dtype=jnp.int32)...  81.3 us
    gather x2, local copies, waits for them, and re-layouts, shards(): by_target = jnp.take(stacked, slot_table, axis=3).transpose(3, 0, 1, 2, 4)  74.6 us
    slice x15, local copies, waits for them, and re-layouts, transport(): forward = jnp.roll(values, -1, axis=0)  62.9 us
    reduce_sum x2, other arithmetic, cloud_model(): ground_precipitation = ground_precipitation + jnp.mean(condensed, axis=0)  46.8 us
    gather x2, local copies, waits for them, and re-layouts, shards(): column_tend = jnp.take(in_slot_order, inverse, axis=2)  36.6 us
    scatter x1, local copies, waits for them, and re-layouts, shards(): inverse = jnp.zeros((block_cols,), jnp.int32).at[slot_list].set(jnp.arang...  34.2 us
    all_to_all x1, waiting for transfers between devices, shards(): lax.all_to_all(fields_now, 'col', split_axis=1, concat_axis=3, tiled=True)  31.7 us
    all_to_all x1, blocking collectives, shards(): lax.all_to_all(outgoing, ('sec', 'lat'), split_axis=0, concat_axis=1, til...  30.3 us
  transfers between devices with their start and end apart: 3, of which 1 were waited for; matrix products, arithmetic and copies ran while one was open for 19% of the time, Pallas kernels for 0%

commit v1 on v0

--- a/solution.py
+++ b/solution.py
@@ -140,7 +140,10 @@
         column_tend = jnp.take(in_slot_order, inverse, axis=2)
     new_state = state + column_tend.reshape(members, 1, levels, band_rows, lon_block)
     fields_now = new_state[:, 0]
-    regrouped = lax.all_to_all(fields_now, "col", split_axis=1, concat_axis=3, tiled=True)
+    regrouped = jnp.concatenate(
+        lax.all_to_all(jnp.stack(jnp.split(fields_now, lax.axis_size("col"), axis=1)), "col", 0, 0),
+        axis=3,
+    )
     trig_rows = trig_table(jnp.arange(NLON, dtype=jnp.int32), wave_table)
     spectra = jnp.einsum("elay,ycs->leacs", regrouped, trig_rows, precision=lax.Precision.HIGHEST)
     owner_count = MMAX // lat_bands

time: 625 us -> 602 us (0.963)
  other arithmetic: 175 us -> 147 us
    sqrt x32, other arithmetic: 20.6 us -> 0.77 us  [march_forward(): jnp.sqrt(numerator / bottom) * (cosine * current - retreat * previous)]
    sqrt x16, other arithmetic: 10.4 us -> 0.44 us  [march_forward(): jnp.sqrt(jnp.maximum(lower_deg * lower_deg - order_col * order_col, 0.0)...]
  transfers between devices with their start and end apart: 3 -> 3, of which waited for: 1 -> 1; matrix products, arithmetic and copies ran while one was open for 19% -> 15% of each run, Pallas kernels for 0% -> 0%
where the time goes in v1:
time: 602 us; the launch traced here: 595 us
  local copies, waits for them, and re-layouts  282 us (47%)
  other arithmetic  147 us (24%)
  loops' own time  80.2 us (13%)
  waiting for transfers between devices  32.3 us (5%)
  blocking collectives  30.3 us (5%)
  starting transfers between devices  12.3 us (2%)
  matrix products  10.2 us (2%)
    another operation x1, loops' own time, legendre_table(): lax.scan(march_forward, (empty, empty), jnp.arange(MMAX, dtype=jnp.int32)...  80.2 us
    gather x2, local copies, waits for them, and re-layouts, shards(): by_target = jnp.take(stacked, slot_table, axis=3).transpose(3, 0, 1, 2, 4)  74.6 us
    slice x15, local copies, waits for them, and re-layouts, transport(): forward = jnp.roll(values, -1, axis=0)  62.9 us
    reduce_sum x2, other arithmetic, cloud_model(): ground_precipitation = ground_precipitation + jnp.mean(condensed, axis=0)  46.8 us
    gather x2, local copies, waits for them, and re-layouts, shards(): column_tend = jnp.take(in_slot_order, inverse, axis=2)  37.5 us
    scatter x1, local copies, waits for them, and re-layouts, shards(): inverse = jnp.zeros((block_cols,), jnp.int32).at[slot_list].set(jnp.arang...  34.2 us
    all_to_all x1, waiting for transfers between devices, shards(): lax.all_to_all(jnp.stack(jnp.split(fields_now, lax.axis_size('col'), axis...  32.3 us
    all_to_all x1, blocking collectives, shards(): lax.all_to_all(outgoing, ('sec', 'lat'), split_axis=0, concat_axis=1, til...  30.3 us
  transfers between devices with their start and end apart: 3, of which 1 were waited for; matrix products, arithmetic and copies ran while one was open for 15% of the time, Pallas kernels for 0%

profile of v1, /device:TPU:0, one launch (start us, length us, event | category | flops | bytes accessed | tf_op | source)
XLA Modules:
  0.0 595.5 jit_solution(8140534007367251549)
XLA Ops:
  0.6 4.0 copy.116
  4.6 4.1 copy.117
  8.8 12.9 %maximum_bitcast_fusion = f32[2,28,9216]{1,0,2:T(2,128)} fusion(f32[1,1,28,9216]{2,0,3,1:T(1,128)} %bitcast.290, f32[1,1,28,9216]{2,0,3,1:T(1,128)} %bitcast.289), kind=kLoop, calls=%fused_computation.84 | loop fusion | flops 516096 | bytes 4128768 | tf_op jit(solution)/shard_map/stack | solution.py:103
  21.7 66.6 %gather_fusion = f32[9216,2,28]{2,1,0:T(2,128)} fusion(f32[2,28,9216]{1,0,2:T(2,128)} %maximum_bitcast_fusion, s32[9216]{0:T(1024)S(1)} %broadcast_clamp_fusion), kind=kCustom, calls=%fused_computation | custom fusion | bytes 4165632 | tf_op jit(solution)/shard_map/jit(_take)/gather | solution.py:114
  88.3 8.0 %copy.118 = f32[8,1152,2,28]{1,0,2,3:T(8,128)S(1)} copy(f32[8,1152,2,28]{3,2,1,0:T(2,128)} %bitcast.291) | data formatting | bytes 4128768 | tf_op jit(solution)/shard_map/jit(_take)/gather | solution.py:114
  97.9 2.1 copy.96
  100.0 30.3 %all_to_all.38 = f32[8,1,64512]{2,1,0:T(1,128)S(1)} all-to-all(f32[8,1,64512]{2,1,0:T(1,128)S(1)} %copy.96), channel_id=1, replica_groups=mesh['sec'=4,'lat'=2,'col'=4] {'sec','lat'}, dimensions={0} | all-to-all | bytes 4128768 | tf_op jit(solution)/shard_map/all_to_all | solution.py:117
  130.3 6.9 %reduce.8 = f32[8,64512]{1,0:T(8,128)} reduce(f32[8,1,64512]{2,1,0:T(1,128)S(1)} %all_to_all.38, f32[]{:T(128)} %constant.239), dimensions={1}, to_apply=%all_to_all.12.reduce_sub_computation | reduce | bytes 4128772 | tf_op jit(solution)/shard_map/all_to_all | solution.py:117
  137.2 2.0 reshape.4363
  140.2 1.0 squeeze.69
  141.2 1.8 broadcast_multiply_fusion.3
  143.9 1.8 copy.98
  145.6 2.2 squeeze.70
  147.9 0.9 slice_multiply_fusion.1
  148.8 1.8 copy_bitcast_fusion.2
  151.3 8.7 %fusion.44 = (f32[1,32,28,2304]{3,1,2,0:T(8,128)}, f32[1,32,28,2304]{3,1,2,0:T(8,128)S(1)}) fusion(f32[1,1,28,2304]{3,1,2,0:T(1,128)S(1)} %get-tuple-element.416, f32[1,31,28,2304]{3,1,2,0:T(8,128)S(1)} %slice.206, bf16[1,32,28,1,1,2304]{5,1,4,3,2,0:T(8,128)(2,1)S(1)} %copy-done.2, f32[28,2304]{1,0:T(8,128)S(1)} %get-tuple-element.422, ...), kind=kLoop, calls=%fused_computation.94 | loop fusion | flops 33030144 | bytes 30449664 | tf_op jit(solution)/shard_map/vmap()/add | solution.py:37
  160.1 6.4 %fusion.107 = (f32[1,31,28,2304]{3,1,2,0:T(8,128)}, f32[1,31,28,2304]{3,1,2,0:T(8,128)}) fusion(f32[1,32,28,2304]{3,1,2,0:T(8,128)S(1)} %get-tuple-element.407), kind=kLoop, calls=%fused_computation.241 | loop fusion | bytes 31997952 | tf_op jit(solution)/shard_map/vmap(jit(_roll_static))/slice | solution.py:16
  166.9 15.7 %fusion.51 = (f32[28,2304]{1,0:T(8,128)}, f32[28,2304]{1,0:T(8,128)}, f32[1,32,28,2304]{3,1,2,0:T(8,128)S(1)}) fusion(f32[28,2304]{1,0:T(8,128)S(1)} %get-tuple-element.422, bf16[1,32,28,1,1,2304]{5,1,4,3,2,0:T(8,128)(2,1)S(1)} %copy-done.2, f32[28,2304]{1,0:T(8,128)S(1)} %get-tuple-element.427, f32[28,2304]{1,0:T(8,128)S(1)} %copy-done.9, ...), kind=kLoop, calls=%fused_computation.125 | loop fusion | flops 67995648 | bytes 39481344 | tf_op jit(solution)/shard_map/vmap()/reduce_sum | solution.py:40
  182.6 8.4 %fusion.105 = (f32[1,31,28,2304]{3,1,2,0:T(8,128)}, f32[1,31,28,2304]{3,1,2,0:T(8,128)}) fusion(f32[1,32,28,2304]{3,1,2,0:T(8,128)S(1)} %get-tuple-element.336), kind=kLoop, calls=%fused_computation.239 | loop fusion | bytes 31997952 | tf_op jit(solution)/shard_map/vmap(jit(_roll_static))/slice | solution.py:16
  191.0 2.2 copy-done
  193.2 1.1 fusion.106
  194.4 6.4 %fusion.103 = (f32[1,31,28,2304]{3,1,2,0:T(8,128)}, f32[1,31,28,2304]{3,1,2,0:T(8,128)}) fusion(f32[1,32,28,2304]{3,1,2,0:T(8,128)S(1)} %bitcast.287), kind=kLoop, calls=%fused_computation.237 | loop fusion | bytes 31997952 | tf_op jit(solution)/shard_map/vmap(jit(_roll_static))/slice | solution.py:16
  200.7 1.2 fusion.104
  201.9 31.1 %fusion.52 = (f32[28,2304]{1,0:T(8,128)}, f32[1,32,28,2304]{3,1,2,0:T(8,128)}, f32[1,32,28,2304]{3,1,2,0:T(8,128)}) fusion(f32[28,2304]{1,0:T(8,128)S(1)} %get-tuple-element.423, f32[1,32,28,2304]{3,1,2,0:T(8,128)} %copy-done, f32[28,2304]{1,0:T(8,128)S(1)} %get-tuple-element.422, bf16[1,32,28,1,1,2304]{5,1,4,3,2,0:T(8,128)(2,1)S(1)} %copy-done.2, ...), kind=kLoop, calls=%fused_computation.126 | loop fusion | flops 96961536 | bytes 72253440 | tf_op jit(solution)/shard_map/vmap()/reduce_sum | solution.py:40
  233.0 12.5 %fusion.97 = (f32[1,31,28,2304]{3,1,2,0:T(8,128)}, f32[1,31,28,2304]{3,1,2,0:T(8,128)}) fusion(f32[1,32,28,2304]{3,1,2,0:T(8,128)} %get-tuple-element.338), kind=kLoop, calls=%fused_computation.231 | loop fusion | bytes 31997952 | tf_op jit(solution)/shard_map/vmap(jit(_roll_static))/slice | solution.py:16
  245.5 3.3 fusion.98
  248.9 6.4 %fusion.101 = (f32[1,31,28,2304]{3,1,2,0:T(8,128)}, f32[1,31,28,2304]{3,1,2,0:T(8,128)}) fusion(f32[1,32,28,2304]{3,1,2,0:T(8,128)S(1)} %bitcast.285), kind=kLoop, calls=%fused_computation.235 | loop fusion | bytes 31997952 | tf_op jit(solution)/shard_map/vmap(jit(_roll_static))/slice | solution.py:16
  255.2 1.1 fusion.102
  256.4 18.1 %subtract_add_fusion = (f32[1,32,28,2304]{3,1,2,0:T(8,128)S(1)}, f32[1,32,28,2304]{3,1,2,0:T(8,128)S(1)}) fusion(f32[1,32,28,2304]{3,1,2,0:T(8,128)} %get-tuple-element.338, f32[1,31,28,2304]{3,1,2,0:T(8,128)} %get-tuple-element.383, f32[1,1,28,2304]{3,1,2,0:T(1,128)} %get-tuple-element.385, f32[1,1,28,2304]{3,1,2,0:T(1,128)} %get-tuple-element.384, ...), kind=kLoop, calls=%fused_computation.114 | loop fusion | flops 55738368 | bytes 67092480 | tf_op jit(solution)/shard_map/vmap()/add | solution.py:39
  274.5 6.4 %fusion.95 = (f32[1,31,28,2304]{3,1,2,0:T(8,128)}, f32[1,31,28,2304]{3,1,2,0:T(8,128)}) fusion(f32[1,32,28,2304]{3,1,2,0:T(8,128)S(1)} %get-tuple-element.376), kind=kLoop, calls=%fused_computation.229 | loop fusion | bytes 31997952 | tf_op jit(solution)/shard_map/vmap(jit(_roll_static))/slice | solution.py:16
  280.9 1.1 fusion.96
  282.0 6.4 %fusion.99 = (f32[1,31,28,2304]{3,1,2,0:T(8,128)}, f32[1,31,28,2304]{3,1,2,0:T(8,128)}) fusion(f32[1,32,28,2304]{3,1,2,0:T(8,128)S(1)} %get-tuple-element.377), kind=kLoop, calls=%fused_computation.233 | loop fusion | bytes 31997952 | tf_op jit(solution)/shard_map/vmap(jit(_roll_static))/slice | solution.py:16
  288.4 1.2 fusion.100
  289.6 20.4 %add_reduce_fusion = (f32[28,2304]{1,0:T(8,128)}, f32[28,2304]{1,0:T(8,128)}, f32[28,2304]{1,0:T(8,128)}) fusion(f32[1,32,28,2304]{3,1,2,0:T(8,128)S(1)} %get-tuple-element.377, f32[1,31,28,2304]{3,1,2,0:T(8,128)} %get-tuple-element.387, f32[1,1,28,2304]{3,1,2,0:T(1,128)} %get-tuple-element.389, f32[1,1,28,2304]{3,1,2,0:T(1,128)} %get-tuple-element.388, ...), kind=kLoop, calls=%fused_computation.111 | loop fusion | flops 67931136 | bytes 55738368 | tf_op jit(solution)/shard_map/vmap()/reduce_sum | solution.py:44
  310.0 1.0 broadcast_multiply_fusion.1
  311.0 1.3 multiply_negate_fusion
  312.3 4.1 fusion.64
  317.3 2.0 reshape.4411
  319.3 3.6 all-to-all-start.1
  322.9 34.2 %scatter_custom_fusion = s32[9216]{0:T(1024)S(1)} fusion(s32[9216]{0:T(1024)S(1)} %bitcast.313, s32[9216]{0:T(1024)S(1)} %iota.45, s32[]{:T(128)} %constant.186.clone.1), kind=kCustom, calls=%fused_computation.183 | custom fusion | bytes 36868 | tf_op jit(solution)/shard_map/scatter | solution.py:138
  357.4 3.4 copy.105
  360.8 33.5 %gather_fusion.1 = f32[9216,28]{1,0:T(8,128)} fusion(f32[28,9216]{0,1:T(8,128)} %bitcast.288, s32[9216]{0:T(1024)S(1)} %fusion.73), kind=kCustom, calls=%fused_computation.1 | custom fusion | bytes 2101248 | tf_op jit(solution)/shard_map/jit(_take)/gather | solution.py:140
  394.3 4.0 copy.106
  398.3 1.5 select_add_fusion
  399.9 1.3 pad_maximum_fusion.15
  401.3 5.1 all-to-all-start.2
  407.5 32.3 %all-to-all-done.2 = f32[4,1,7,96,96]{4,3,2,1,0:T(8,128)} async-done(((f32[4,1,7,96,96]{4,3,2,1,0:T(8,128)}), f32[4,1,7,96,96]{4,3,2,1,0:T(8,128)}, u32[]{:S(2)}, u32[]{:S(2)}) %all-to-all-start.2) | async-done | bytes 1032224 | tf_op jit(solution)/shard_map/all_to_all | solution.py:144
  439.8 3.3 copy.108
  443.1 2.9 reshape.4409
  446.0 2.5 convolution_bitcast_fusion
  448.5 1.4 copy.109
  449.9 3.6 all-to-all-start.3
  453.5 122.8 %while.19 = (s32[]{:T(128)}, f32[64,192]{1,0:T(8,128)S(1)}, f32[64,192]{1,0:T(8,128)S(1)}, f32[16,8,64,192]{3,2,1,0:T(8,128)}, s32[16,8]{0,1:T(8,128)S(1)}, /*in...) while((s32[]{:T(128)}, f32[64,192]{1,0:T(8,128)S(1)}, ...), condition=%wide.region_8.9_spmd.clone.clone, body=%wide.region_7.8_spmd.clone.clone.sunk | while | flops 926866 | bytes 3029748 | solution.py:85
  467.9 0.9 bitcast_dynamic-update-slice_fusion.26
  490.9 0.9 bitcast_dynamic-update-slice_fusion.26
  513.9 0.9 bitcast_dynamic-update-slice_fusion.26
  521.6 0.9 bitcast_dynamic-update-slice_fusion.26
  529.3 0.9 bitcast_dynamic-update-slice_fusion.26
  544.6 0.9 bitcast_dynamic-update-slice_fusion.26
  567.6 0.9 bitcast_dynamic-update-slice_fusion.26
  575.3 0.9 bitcast_dynamic-update-slice_fusion.26
  576.2 8.6 %copy.107 = f32[128,64,192]{0,2,1:T(8,128)} copy(f32[128,64,192]{2,1,0:T(8,128)} %bitcast.293) | data formatting | bytes 12582912 | tf_op jit(solution)/shard_map/reshape | solution.py:85
  586.3 7.7 %fusion.56 = f32[1,1,7,64,2,128]{5,2,4,3,1,0:T(8,128)S(1)} fusion(f32[7,192,2,64]{1,0,2,3:T(8,128)S(1)} %reshape.4413, f32[128,64,192]{0,2,1:T(8,128)} %copy.107, f32[192]{0:T(256)S(1)} %fusion.76), kind=kOutput, calls=%fused_computation.134 | convolution fusion | flops 265814016 | bytes 7439104 | tf_op jit(solution)/shard_map/leacs,nsa->lescn/dot_general | solution.py:154
  594.0 1.0 copy.113
  (335 shorter events, 43.7 us)
Async XLA Ops:
  0.6 8.1 %copy-start.12 = (s32[1,1,9216]{2,1,0:T(1,128)S(1)}, s32[1,1,9216]{2,1,0:T(1,128)}, u32[]{:S(2)}) copy-start(s32[1,1,9216]{2,1,0:T(1,128)} %param.10) | copy-start | bytes 110596
  141.2 2.6 copy-start.5
  143.8 58.1 %copy-start.3 = (f32[28,2304]{1,0:T(8,128)}, f32[28,2304]{1,0:T(8,128)S(1)}, u32[]{:S(2)}) copy-start(f32[28,2304]{1,0:T(8,128)S(1)} %get-tuple-element.427) | copy-start | bytes 774148
  143.8 7.5 %copy-start.9 = (f32[28,2304]{1,0:T(8,128)S(1)}, f32[28,2304]{1,0:T(8,128)}, u32[]{:S(2)}) copy-start(f32[28,2304]{1,0:T(8,128)} %broadcast_multiply_fusion.2) | copy-start | bytes 774148
  147.8 1.0 copy-start.10
  147.8 3.5 copy-start.2
  151.3 15.6 %copy-start.1 = (f32[1,31,28,2304]{3,1,2,0:T(8,128)}, f32[1,31,28,2304]{3,1,2,0:T(8,128)S(1)}, u32[]{:S(2)}) copy-start(f32[1,31,28,2304]{3,1,2,0:T(8,128)S(1)} %slice.206) | copy-start | bytes 23998468
  182.6 10.6 %copy-start = (f32[1,32,28,2304]{3,1,2,0:T(8,128)}, f32[1,32,28,2304]{3,1,2,0:T(8,128)S(1)}, u32[]{:S(2)}) copy-start(f32[1,32,28,2304]{3,1,2,0:T(8,128)S(1)} %get-tuple-element.336) | copy-start | bytes 24772612
  182.6 11.8 %slice-start.2 = ((s8[8257536]{0:T(1024)(128)(4,1)}), s8[4194304]{0:T(1024)(128)(4,1)S(1)}, s32[]{:S(2)}) async-start(s8[8257536]{0:T(1024)(128)(4,1)} %bitcast.286), calls=%async_computation.6 | async-start | bytes 8388608
  182.6 11.8 %slice-start.3 = ((s8[8257536]{0:T(1024)(128)(4,1)}), s8[4063232]{0:T(1024)(128)(4,1)S(1)}, s32[]{:S(2)}) async-start(s8[8257536]{0:T(1024)(128)(4,1)} %bitcast.286), calls=%async_computation.7 | async-start | bytes 8126464
  233.0 15.8 %slice-start = ((s8[8257536]{0:T(1024)(128)(4,1)}), s8[4194304]{0:T(1024)(128)(4,1)S(1)}, s32[]{:S(2)}) async-start(s8[8257536]{0:T(1024)(128)(4,1)} %bitcast.284), calls=%async_computation.4 | async-start | bytes 8388608
  233.0 15.8 %slice-start.1 = ((s8[8257536]{0:T(1024)(128)(4,1)}), s8[4063232]{0:T(1024)(128)(4,1)S(1)}, s32[]{:S(2)}) async-start(s8[8257536]{0:T(1024)(128)(4,1)} %bitcast.284), calls=%async_computation.5 | async-start | bytes 8126464
  282.0 7.6 %copy-start.4 = (f32[28,2304]{1,0:T(8,128)S(1)}, f32[28,2304]{1,0:T(8,128)}, u32[]{:S(2)}) copy-start(f32[28,2304]{1,0:T(8,128)} %copy-done.3) | copy-start | bytes 774148
  289.6 22.7 %copy-start.6 = (f32[1,4,28,2304]{3,1,2,0:T(4,128)S(1)}, f32[1,4,28,2304]{3,1,2,0:T(4,128)}, u32[]{:S(2)}) copy-start(f32[1,4,28,2304]{3,1,2,0:T(4,128)} %copy-done.5) | copy-start | bytes 3096580
  310.0 7.0 %copy-start.11 = (f32[28,2304]{1,0:T(8,128)S(1)}, f32[28,2304]{1,0:T(8,128)}, u32[]{:S(2)}) copy-start(f32[28,2304]{1,0:T(8,128)} %get-tuple-element.275) | copy-start | bytes 774148
  310.0 12.9 %copy-start.13 = (s32[1,1,9216]{2,1,0:T(1,128)S(1)}, s32[1,1,9216]{2,1,0:T(1,128)}, u32[]{:S(2)}) copy-start(s32[1,1,9216]{2,1,0:T(1,128)} %param.10) | copy-start | bytes 110596
  319.3 38.0 %all-to-all-start.1 = ((f32[8,1,32256]{2,1,0:T(1,128)}), f32[8,1,32256]{2,1,0:T(1,128)S(1)}, u32[]{:S(2)}, u32[]{:S(2)}) async-start(f32[8,1,32256]{2,1,0:T(1,128)} %reshape.4411), calls=%async_computation.1 | async-start | bytes 2064384 | tf_op jit(solution)/shard_map/all_to_all | solution.py:127
  360.8 37.5 %copy-start.7 = (f32[1,1,28,96,96]{4,3,2,1,0:T(8,128)S(1)}, f32[1,1,28,96,96]{4,3,2,1,0:T(8,128)}, u32[]{:S(2)}) copy-start(f32[1,1,28,96,96]{4,3,2,1,0:T(8,128)} %param.7) | copy-start | bytes 3096580
  394.3 12.2 %copy-start.14 = (s32[128]{0:T(128)S(1)}, s32[128]{0:T(128)}, u32[]{:S(2)}) copy-start(s32[128]{0:T(128)} %param.11) | copy-start | bytes 1540
  399.8 50.1 %copy-start.8 = (f32[1,1,28,96,96]{4,3,2,1,0:T(8,128)}, f32[1,1,28,96,96]{4,3,2,1,0:T(8,128)S(1)}, u32[]{:S(2)}) copy-start(f32[1,1,28,96,96]{4,3,2,1,0:T(8,128)S(1)} %select_add_fusion) | copy-start | bytes 3096580
  401.3 38.5 %all-to-all-start.2 = ((f32[4,1,7,96,96]{4,3,2,1,0:T(8,128)}), f32[4,1,7,96,96]{4,3,2,1,0:T(8,128)}, u32[]{:S(2)}, u32[]{:S(2)}) async-start(f32[4,1,7,96,96]{4,3,2,1,0:T(8,128)} %pad_maximum_fusion.15), calls=%async_computation.2 | async-start | bytes 2752512 | tf_op jit(solution)/shard_map/all_to_all | solution.py:144
  449.9 135.0 %all-to-all-start.3 = ((f32[7,1,96,2,128]{2,3,1,0,4:T(2,128)}), f32[7,1,96,2,128]{2,3,1,0,4:T(2,128)S(1)}, u32[]{:S(2)}, u32[]{:S(2)}) async-start(f32[7,1,96,2,128]{2,3,1,0,4:T(2,128)} %copy.109), calls=%async_computation.3 | async-start | bytes 1835008 | tf_op jit(solution)/shard_map/all_to_all | solution.py:156
